TPU v7x, 32 devices: a whole 2x2x4 slice. The times are simulated.
32 devices in a mesh: col: 8 (over y, x, core), dev: 4 (over z).
Axes of the slice: x: 2, y: 2, z: 4, core: 2. Of those that a mesh axis runs over, the one named last changes fastest.
Arguments:
- first_factor: bfloat16 [16, 1024, 2048], P(None, 'col', 'dev'), may hold values from -1 to 1
- second_factor: bfloat16 [16, 1024, 2048], P(None, 'dev', 'col'), may hold values from -1 to 1
- amplitudes: bfloat16 [512, 1024, 1024], P(None, 'col', 'dev'), may hold values from -0.0059814453 to 0.0059814453
Outputs:
- ladder: float32 [512, 256], P(('col', 'dev'))
All inputs are finite; a program needn't handle non-finite values.
Results may differ from a plain program's by a relative error of at most 0.0029.
Values may be sent and summed in bfloat16 or wider, within the bound.
A program may use at most 128 MiB of HBM per device.

v0:
```python
import jax
import jax.numpy as jnp
from jax import lax
from jax.sharding import PartitionSpec as P


def on_device(first_factor, second_factor, amplitudes):
    width_a, block_c, _ = first_factor.shape
    width_b, block_d, _ = second_factor.shape
    pairs = amplitudes.shape[0]
    first_whole = lax.all_gather(first_factor, "dev", axis=2, tiled=True).reshape(
        width_a * block_c, -1
    )
    second_whole = lax.all_gather(second_factor, "col", axis=2, tiled=True).reshape(
        width_b * block_d, -1
    )
    tile_sum = lax.dot_general(
        first_whole, second_whole, (((1,), (1,)), ((), ())), preferred_element_type=jnp.float32
    )
    tile = tile_sum.astype(jnp.bfloat16).reshape(width_a, block_c, width_b, block_d)
    partial_value = jnp.einsum(
        "acbd,pcd->pab", tile, amplitudes, preferred_element_type=jnp.float32
    )
    partial_value = partial_value.reshape(pairs, width_a * width_b)
    halfway = lax.psum_scatter(partial_value, "col", scatter_dimension=0, tiled=True)
    return lax.psum_scatter(halfway, "dev", scatter_dimension=0, tiled=True)


def solution(mesh):
    placed = (P(None, "col", "dev"), P(None, "dev", "col"), P(None, "col", "dev"))
    return jax.shard_map(
        on_device, mesh=mesh, in_specs=placed, out_specs=P(("col", "dev"), None), check_vma=False
    )
```

profile of v0, /device:TPU:0, one launch (start us, length us, event | category | flops | bytes accessed | tf_op | source)
XLA Modules:
  0.0 409.0 jit_solution(3210589852640393744)
XLA Ops:
  6.5 0.0 all-gather.3.cloned.1.call-start
  6.5 0.7 all-gather.3.cloned.1.call-update
  7.3 0.0 all-gather.5.cloned.1.call-start
  7.3 0.7 all-gather.5.cloned.1.call-update
  8.0 0.0 reduce-scatter.3.cloned.1.call-start
  8.1 153.2 %all-gather.3.cloned.1.call-done = bf16[16,128,2048]{2,1,0:T(8,128)(2,1)} async-done(((bf16[16,128,512]{2,1,0:T(8,128)(2,1)}), bf16[16,128,2048]{2,1,0:T(8,128)(2,1)}) %all-gather.3.cloned.1.call-update) | async-done | bytes 8388624 | tf_op jit(solution)/shard_map/all_gather | solution.py:11
  161.3 93.1 %all-gather.5.cloned.1.call-done = bf16[16,256,2048]{2,1,0:T(8,128)(2,1)} async-done(((bf16[16,256,256]{2,1,0:T(8,128)(2,1)}), bf16[16,256,2048]{2,1,0:T(8,128)(2,1)}) %all-gather.5.cloned.1.call-update) | async-done | bytes 16777232 | tf_op jit(solution)/shard_map/all_gather | solution.py:14
  254.4 40.6 %convolution_convert_fusion = bf16[2048,4096]{1,0:T(8,128)(2,1)S(1)} fusion(bf16[2048,2048]{1,0:T(8,128)(2,1)} %bitcast.24, bf16[4096,2048]{1,0:T(8,128)(2,1)} %bitcast.23), kind=kOutput, calls=%fused_computation.4 | convolution fusion | flops 34368126976 | bytes 41943040 | tf_op jit(solution)/shard_map/dot_general | solution.py:17
  295.0 8.7 %copy.7 = bf16[256,8,16,256]{3,2,1,0:T(8,128)(2,1)} copy(bf16[256,8,16,256]{3,1,2,0:T(8,128)(2,1)S(1)} %bitcast.20) | data formatting | bytes 33554432
  303.8 42.0 %fusion = f32[16,16,512,1]{2,1,3,0:T(8,128)S(1)} fusion(bf16[512,128,256]{2,1,0:T(8,128)(2,1)} %param.5, bf16[16,128,16,256]{3,2,1,0:T(8,128)(2,1)} %bitcast.21), kind=kOutput, calls=%fused_computation | convolution fusion | flops 8589934592 | bytes 50855936 | tf_op jit(solution)/shard_map/acbd,pcd->pab/dot_general | solution.py:21
  345.7 1.0 copy.5
  346.7 0.0 reduce-scatter.3.cloned.1.call-update
  346.8 0.0 reduce-scatter.5.cloned.1.call-start
  346.8 34.2 %reduce-scatter.3.cloned.1.call-done = f32[64,256]{1,0:T(8,128)} async-done(((f32[512,256]{1,0:T(8,128)}), f32[64,256]{1,0:T(8,128)}) %reduce-scatter.3.cloned.1.call-update) | async-done | bytes 65552 | tf_op jit(solution)/shard_map/reduce_scatter | solution.py:25
  381.0 0.0 reduce-scatter.5.cloned.1.call-update
  381.1 21.4 %reduce-scatter.5.cloned.1.call-done = f32[16,256]{1,0:T(8,128)} async-done(((f32[64,256]{1,0:T(8,128)}), f32[16,256]{1,0:T(8,128)}) %reduce-scatter.5.cloned.1.call-update) | async-done | bytes 16400 | tf_op jit(solution)/shard_map/reduce_scatter | solution.py:26
Async XLA Ops:
  6.5 154.7 %all-gather.3.cloned.1.call-start = ((), (), s32[]{:S(2)}) async-start(), calls=%async_computation.2 | async-start | bytes 10485760 | tf_op jit(solution)/shard_map/all_gather | solution.py:11
  7.3 247.1 %all-gather.5.cloned.1.call-start = ((), (), s32[]{:S(2)}) async-start(), calls=%async_computation.3 | async-start | bytes 18874368 | tf_op jit(solution)/shard_map/all_gather | solution.py:14
  8.0 373.0 %reduce-scatter.3.cloned.1.call-start = ((), (), s32[]{:S(2)}) async-start(), calls=%async_computation.4 | async-start | bytes 589824 | tf_op jit(solution)/shard_map/reduce_scatter | solution.py:25
  346.8 55.7 %reduce-scatter.5.cloned.1.call-start = ((), (), s32[]{:S(2)}) async-start(), calls=%async_computation.5 | async-start | bytes 81920 | tf_op jit(solution)/shard_map/reduce_scatter | solution.py:26
Sparse Core Ops, SparseCore 0:
  8.9 152.3 all-gather.2
  163.1 91.1 all-gather.4
  346.9 34.1 reduce-scatter.2
  383.1 19.2 reduce-scatter.4
where the time goes:
time: 409 us
  waiting for transfers between devices  303 us (74%)
  matrix products  82.6 us (20%)
  between operations  13.1 us (3%)
  local copies, waits for them, and re-layouts  9.73 us (2%)
    all_gather x1, waiting for transfers between devices, on_device(): lax.all_gather(first_factor, 'dev', axis=2, tiled=True)  153 us
    all_gather x1, waiting for transfers between devices, on_device(): lax.all_gather(second_factor, 'col', axis=2, tiled=True)  93.1 us
    dot_general x1, matrix products, on_device(): jnp.einsum('acbd,pcd->pab', tile, amplitudes, preferred_element_type=jnp....  42 us
    dot_general x1, matrix products, on_device(): lax.dot_general(first_whole, second_whole, (((1,), (1,)), ((), ())), pref...  40.6 us
    reduce_scatter x1, waiting for transfers between devices, on_device(): lax.psum_scatter(partial_value, 'col', scatter_dimension=0, tiled=True)  34.2 us
    reduce_scatter x1, waiting for transfers between devices, on_device(): return lax.psum_scatter(halfway, 'dev', scatter_dimension=0, tiled=True)  21.4 us
    unnamed x1, local copies, waits for them, and re-layouts  8.73 us
  transfers between devices with their start and end apart: 4, of which 4 were waited for; matrix products, arithmetic and copies ran while one was open for 0% of the time, Pallas kernels for 0%

commit v1 on v0

v1 whole, which is shorter than its diff:
```python
import functools

import jax
import jax.numpy as jnp
from jax import lax
from jax.experimental import pallas as pl
from jax.experimental.pallas import tpu as pltpu
from jax.sharding import PartitionSpec as P

MESH = pl.DeviceIdType.MESH
CHUNKS = 8
AHEAD = 2
NT = (((1,), (1,)), ((), ()))


def kernel(
    ncol, ndev, first, second, amps, out,
    first_all, second_all, raw, turned, tile, total, parts, final, half_sum,
    own_sem, z_send, z_recv, r_send, r_recv, c_send, c_recv, t_sem, s_send, s_recv, d_send, d_recv,
):
    col, dev = lax.axis_index("col"), lax.axis_index("dev")
    n_c, n_a, q_first = first.shape
    n_b, n_d, q_second = second.shape
    pairs = amps.shape[0]
    size = n_c // CHUNKS
    chips = ncol // 2
    far = chips // 2
    core, chip = lax.rem(col, 2), col // 2

    def swap(spot):
        return jnp.where(spot < far, spot, 3 * far - 1 - spot)

    spot = swap(chip)

    def at_spot(offset):
        return swap(lax.rem(spot + offset + 2 * chips, chips)) * 2 + core

    partner = chip * 2 + 1 - core

    barrier = pltpu.get_barrier_semaphore()
    for off in range(1, ncol):
        pl.semaphore_signal(
            barrier, inc=1, device_id={"col": lax.rem(col + off, ncol)}, device_id_type=MESH
        )
    for off in range(1, ndev):
        pl.semaphore_signal(
            barrier, inc=1, device_id={"dev": lax.rem(dev + off, ndev)}, device_id_type=MESH
        )
    pl.semaphore_wait(barrier, ncol + ndev - 2)

    def z_slice(source, k):
        return first_all.at[
            pl.ds(k * size, size), :, pl.ds(pl.multiple_of(source * q_first, q_first), q_first)
        ]

    def z_copy(way, hop, k):
        step = 1 if way == 0 else -1
        source = dev - step * (hop - 1)
        src = first.at[pl.ds(k * size, size)] if hop == 1 else z_slice(source, k)
        return pltpu.make_async_remote_copy(
            src_ref=src,
            dst_ref=z_slice(source, k),
            send_sem=z_send.at[way, hop - 1, k],
            recv_sem=z_recv.at[way, hop - 1, k],
            device_id={"dev": dev + step},
            device_id_type=MESH,
        )

    def z_arrival(way, hop, k):
        step = 1 if way == 0 else -1
        here = z_slice(dev - step * hop, k)
        return pltpu.make_async_copy(here, here, z_recv.at[way, hop - 1, k])

    def sends(way, hop):
        if way == 0:
            return (dev - (hop - 1) >= 0) & (dev + 1 < ndev)
        return (dev + (hop - 1) < ndev) & (dev - 1 >= 0)

    def receives(way, hop):
        return (dev - hop >= 0) if way == 0 else (dev + hop < ndev)

    def z_own(k):
        for way in range(2):
            @pl.when(sends(way, 1))
            def _():
                z_copy(way, 1, k).start()

    def z_round(k):
        @pl.when(k + AHEAD < CHUNKS)
        def _():
            z_own(k + AHEAD)

        for hop in range(1, ndev):
            for way in range(2):
                @pl.when(receives(way, hop))
                def _():
                    z_arrival(way, hop, k).wait()

                if hop + 1 < ndev:
                    @pl.when(sends(way, hop + 1))
                    def _():
                        z_copy(way, hop + 1, k).start()

    wide = n_b // 2

    def p_slice(source, h):
        return second_all.at[
            pl.ds(h * wide, wide), :, pl.ds(pl.multiple_of(source * q_second, q_second), q_second)
        ]

    def p_source(way, hop):
        return at_spot(-hop if way == 0 else hop)

    def r_copy(way, hop, h):
        source = p_source(way, hop - 1)
        src = second.at[pl.ds(h * wide, wide)] if hop == 1 else p_slice(source, h)
        return pltpu.make_async_remote_copy(
            src_ref=src,
            dst_ref=p_slice(source, h),
            send_sem=r_send.at[way, hop - 1, h],
            recv_sem=r_recv.at[way, hop - 1, h],
            device_id={"col": at_spot(1 if way == 0 else -1)},
            device_id_type=MESH,
        )

    def r_arrival(way, hop, h):
        here = p_slice(p_source(way, hop), h)
        return pltpu.make_async_copy(here, here, r_recv.at[way, hop - 1, h])

    def c_copy(way, hop, h):
        source = p_source(way, hop)
        src = second.at[pl.ds(h * wide, wide)] if hop == 0 else p_slice(source, h)
        return pltpu.make_async_remote_copy(
            src_ref=src,
            dst_ref=p_slice(source, h),
            send_sem=c_send.at[way, hop, h],
            recv_sem=c_recv.at[way, hop, h],
            device_id={"col": partner},
            device_id_type=MESH,
        )

    def c_arrival(way, hop, h):
        source = p_source(way, hop) + 1 - 2 * core
        here = p_slice(source, h)
        return pltpu.make_async_copy(here, here, c_recv.at[way, hop, h])

    def travels(way, hop):
        if hop < far:
            return (0, 1) if way == 0 else (1, 0)
        return (way,) if hop == far else ()

    pieces = [
        (way, hop, travels(way, hop)[place])
        for hop in range(1, far + 1)
        for place in range(len(travels(0, hop)))
        for way in range(2)
    ]
    shared = [(0, 0, 0), (0, 0, 1)] + pieces

    own_first = pltpu.make_async_copy(
        first, first_all.at[:, :, pl.ds(pl.multiple_of(dev * q_first, q_first), q_first)],
        own_sem.at[0],
    )
    own_second = pltpu.make_async_copy(
        second, second_all.at[:, :, pl.ds(pl.multiple_of(col * q_second, q_second), q_second)],
        own_sem.at[1],
    )

    def t_copy(k):
        slot = lax.rem(k, 2)
        return pltpu.make_async_copy(
            amps.at[:, pl.ds(pl.multiple_of(k * size, size), size), :], raw.at[slot],
            t_sem.at[slot],
        )

    for k in range(AHEAD):
        z_own(k)
    for way, hop, h in pieces:
        if hop == 1:
            r_copy(way, 1, h).start()
    own_first.start()
    own_second.start()
    t_copy(0).start()
    for h in range(2):
        c_copy(0, 0, h).start()

    lead = CHUNKS // 2
    by_round = [[] for _ in range(lead)]
    for number, piece in enumerate(pieces):
        by_round[min(lead - 1, 1 + number * lead // len(pieces))].append(piece)

    def take(way, hop, h):
        r_arrival(way, hop, h).wait()
        if h in travels(way, hop + 1):
            r_copy(way, hop + 1, h).start()
        c_copy(way, hop, h).start()

    for k in range(lead):
        for piece in by_round[k]:
            take(*piece)
        z_round(k)
    own_first.wait()
    own_second.wait()
    for piece in shared:
        c_arrival(*piece).wait()

    total[...] = jnp.zeros_like(total)

    def one_block(k, _):
        slot = lax.rem(k, 2)
        t_copy(k).wait()

        @pl.when(k + 1 < CHUNKS)
        def _():
            t_copy(k + 1).start()

        def turn(i, _):
            rows = pl.ds(pl.multiple_of(i * 16, 16), 16)
            turned[:, rows, :] = jnp.swapaxes(raw[slot, rows], 0, 1)
            return 0

        lax.fori_loop(0, pairs // 16, turn, 0)

        def one_b(b, _):
            left = first_all[pl.ds(k * size, size)].reshape(size * n_a, -1)
            got = lax.dot_general(left, second_all[b], NT, preferred_element_type=jnp.float32)
            tile[:, b] = got.astype(jnp.bfloat16).reshape(size, n_a, n_d)
            return 0

        lax.fori_loop(0, n_b, one_b, 0)

        def one_c(c, _):
            total[...] += lax.dot_general(
                turned[c], tile[c].reshape(n_b * n_a, n_d), NT, preferred_element_type=jnp.float32
            )
            return 0

        lax.fori_loop(0, size, one_c, 0)

        @pl.when(((lax.rem(k, 2) == 1) & (k < CHUNKS - 1)) | (k == CHUNKS - 2))
        def _():
            z_round(lead + k // 2)

        return 0

    lax.fori_loop(0, CHUNKS, one_block, 0)

    some = pairs // ncol

    def s_copy(off):
        to = lax.rem(col + off, ncol)
        return pltpu.make_async_remote_copy(
            src_ref=total.at[pl.ds(pl.multiple_of(to * some, some), some)],
            dst_ref=parts.at[off],
            send_sem=s_send.at[off],
            recv_sem=s_recv.at[off],
            device_id={"col": to},
            device_id_type=MESH,
        )

    for off in range(1, ncol):
        s_copy(off).start()
    mine = total[pl.ds(pl.multiple_of(col * some, some), some), :]
    for off in range(1, ncol):
        s_copy(off).wait_recv()
        mine += parts[off]
    half_sum[...] = mine.reshape(half_sum.shape)

    def d_copy(off):
        to = lax.rem(dev + off, ndev)
        return pltpu.make_async_remote_copy(
            src_ref=half_sum.at[to],
            dst_ref=final.at[off],
            send_sem=d_send.at[off],
            recv_sem=d_recv.at[off],
            device_id={"dev": to},
            device_id_type=MESH,
        )

    for off in range(1, ndev):
        d_copy(off).start()
    result = half_sum[dev]
    for off in range(1, ndev):
        d_copy(off).wait_recv()
        result += final[off]
    out[...] = result

    for off in range(1, ncol):
        s_copy(off).wait_send()
    for off in range(1, ndev):
        d_copy(off).wait_send()
    for piece in pieces:
        r_copy(*piece).wait_send()
    for piece in shared:
        c_copy(*piece).wait_send()

    def drain(k, _):
        for way in range(2):
            for hop in range(1, ndev):
                @pl.when(sends(way, hop))
                def _():
                    z_copy(way, hop, k).wait_send()
        return 0

    lax.fori_loop(0, CHUNKS, drain, 0)


def on_device(ncol, ndev, first_factor, second_factor, amplitudes):
    n_a, n_c, q_first = first_factor.shape
    n_b, n_d, q_second = second_factor.shape
    pairs = amplitudes.shape[0]
    size = n_c // CHUNKS
    far = ncol // 4
    whole = q_first * ndev
    some = pairs // ncol
    few = some // ndev
    width = n_a * n_b
    anywhere = pl.BlockSpec(memory_space=pl.ANY)
    dma = pltpu.SemaphoreType.DMA
    got = pl.pallas_call(
        functools.partial(kernel, ncol, ndev),
        out_shape=jax.ShapeDtypeStruct((few, width), jnp.float32),
        in_specs=[anywhere] * 3,
        out_specs=pl.BlockSpec(memory_space=pltpu.VMEM),
        scratch_shapes=[
            pltpu.VMEM((n_c, n_a, whole), jnp.bfloat16),
            pltpu.VMEM((n_b, n_d, whole), jnp.bfloat16),
            pltpu.VMEM((2, pairs, size, n_d), jnp.bfloat16),
            pltpu.VMEM((size, pairs, n_d), jnp.bfloat16),
            pltpu.VMEM((size, n_b, n_a, n_d), jnp.bfloat16),
            pltpu.VMEM((pairs, width), jnp.float32),
            pltpu.VMEM((ncol, some, width), jnp.float32),
            pltpu.VMEM((ndev, few, width), jnp.float32),
            pltpu.VMEM((ndev, few, width), jnp.float32),
            dma((2,)),
            dma((2, ndev - 1, CHUNKS)),
            dma((2, ndev - 1, CHUNKS)),
            dma((2, far, 2)),
            dma((2, far, 2)),
            dma((2, far + 1, 2)),
            dma((2, far + 1, 2)),
            dma((2,)),
            dma((ncol,)),
            dma((ncol,)),
            dma((ndev,)),
            dma((ndev,)),
        ],
        compiler_params=pltpu.CompilerParams(
            collective_id=0, has_side_effects=True, vmem_limit_bytes=58 * 2**20
        ),
    )(jnp.swapaxes(first_factor, 0, 1), second_factor, amplitudes)
    return jnp.swapaxes(got.reshape(few, n_b, n_a), 1, 2).reshape(few, width)


def solution(mesh):
    placed = (P(None, "col", "dev"), P(None, "dev", "col"), P(None, "col", "dev"))
    return jax.shard_map(
        functools.partial(on_device, mesh.shape["col"], mesh.shape["dev"]),
        mesh=mesh, in_specs=placed, out_specs=P(("col", "dev"), None), check_vma=False,
    )
```

time: 409 us -> 247 us (0.60)
  waiting for transfers between devices: 303 us -> 0 us
  Pallas kernels: 0 us -> 241 us
  matrix products: 82.6 us -> 0 us
  between operations: 13.1 us -> 0.03 us
    all_gather x2 -> x0, waiting for transfers between devices: 246 us -> none  [the longest x1 153 us: on_device(): lax.all_gather(first_factor, 'dev', axis=2, tiled=True)]
    pallas_call x0 -> x1, Pallas kernels: none -> 241 us  [on_device(): pl.pallas_call(functools.partial(kernel, ncol, ndev), out_shape=jax.Shape...]
    dot_general x2 -> x0, matrix products: 82.6 us -> none  [the longest x1 42 us: on_device(): jnp.einsum('acbd,pcd->pab', tile, amplitudes, preferred_element_type=jnp....]
    reduce_scatter x2 -> x0, waiting for transfers between devices: 55.6 us -> none  [the longest x1 34.2 us: on_device(): lax.psum_scatter(partial_value, 'col', scatter_dimension=0, tiled=True)]
    unnamed x1, local copies, waits for them, and re-layouts: 8.73 us -> 4.1 us
  transfers between devices with their start and end apart: 4 -> 0, of which waited for: 4 -> 0; matrix products, arithmetic and copies ran while one was open for 0% -> 0% of each run, Pallas kernels for 0% -> 0%
where the time goes in v1:
time: 247 us
  Pallas kernels  241 us (98%)
  local copies, waits for them, and re-layouts  5.72 us (2%)
    pallas_call x1, Pallas kernels, on_device(): pl.pallas_call(functools.partial(kernel, ncol, ndev), out_shape=jax.Shape...  241 us

profile of v1, /device:TPU:0, one launch (start us, length us, event | category | flops | bytes accessed | tf_op | source)
XLA Modules:
  0.0 247.1 jit_solution(3751217522157419152)
XLA Ops:
  0.0 4.1 %copy.7 = bf16[16,128,512]{2,0,1:T(8,128)(2,1)} copy(bf16[16,128,512]{2,1,0:T(8,128)(2,1)} %param.3) | data formatting | bytes 4194304 | tf_op args[0]
  4.1 241.4 %shard_map.37 = f32[16,256]{1,0:T(8,128)} custom-call(bf16[128,16,512]{2,1,0:T(8,128)(2,1)} %bitcast.4, bf16[16,256,256]{2,1,0:T(8,128)(2,1)} %second.1, bf16[512,128,256]{2,1,0:T(8,128)(2,1)} %amps.1), custom_call_target="tpu_custom_call" | custom-call | tf_op jit(solution)/shard_map/pallas_call | solution.py:320
  245.5 0.8 reshape.6
  246.3 0.1 copy.5
  246.4 0.7 reshape.7

commit v2 on v1

--- a/solution.py
+++ b/solution.py
@@ -10,6 +10,8 @@
 MESH = pl.DeviceIdType.MESH
 CHUNKS = 8
 AHEAD = 2
+GROUP = 8
+WIDE = 8
 NT = (((1,), (1,)), ((), ()))
 
 
@@ -195,7 +197,23 @@
             r_copy(way, hop + 1, h).start()
         c_copy(way, hop, h).start()
 
+    def turn_block(k):
+        slot, held = lax.rem(k, 2), lax.rem(k, lead)
+        t_copy(k).wait()
+
+        @pl.when(k + 1 < CHUNKS)
+        def _():
+            t_copy(k + 1).start()
+
+        def turn(i, _):
+            rows = pl.ds(pl.multiple_of(i * 16, 16), 16)
+            turned[held, :, rows, :] = jnp.swapaxes(raw[slot, rows], 0, 1)
+            return 0
+
+        lax.fori_loop(0, pairs // 16, turn, 0)
+
     for k in range(lead):
+        turn_block(k)
         for piece in by_round[k]:
             take(*piece)
         z_round(k)
@@ -207,35 +225,31 @@
     total[...] = jnp.zeros_like(total)
 
     def one_block(k, _):
-        slot = lax.rem(k, 2)
-        t_copy(k).wait()
-
-        @pl.when(k + 1 < CHUNKS)
-        def _():
-            t_copy(k + 1).start()
-
-        def turn(i, _):
-            rows = pl.ds(pl.multiple_of(i * 16, 16), 16)
-            turned[:, rows, :] = jnp.swapaxes(raw[slot, rows], 0, 1)
-            return 0
-
-        lax.fori_loop(0, pairs // 16, turn, 0)
+        held = lax.rem(k, lead)
 
         def one_b(b, _):
             left = first_all[pl.ds(k * size, size)].reshape(size * n_a, -1)
-            got = lax.dot_general(left, second_all[b], NT, preferred_element_type=jnp.float32)
-            tile[:, b] = got.astype(jnp.bfloat16).reshape(size, n_a, n_d)
+            right = second_all[pl.ds(b * WIDE, WIDE)].reshape(WIDE * n_d, -1)
+            got = lax.dot_general(left, right, NT, preferred_element_type=jnp.float32)
+            got = got.astype(jnp.bfloat16)
+            for i in range(WIDE):
+                tile[:, b * WIDE + i] = got[:, i * n_d : (i + 1) * n_d].reshape(size, n_a, n_d)
             return 0
 
-        lax.fori_loop(0, n_b, one_b, 0)
-
-        def one_c(c, _):
-            total[...] += lax.dot_general(
-                turned[c], tile[c].reshape(n_b * n_a, n_d), NT, preferred_element_type=jnp.float32
-            )
+        lax.fori_loop(0, n_b // WIDE, one_b, 0)
+
+        def some_c(g, _):
+            group = [g * GROUP + i for i in range(GROUP)]
+            left = jnp.concatenate([turned[held, c] for c in group], axis=1)
+            right = jnp.concatenate([tile[c].reshape(n_b * n_a, n_d) for c in group], axis=1)
+            total[...] += lax.dot_general(left, right, NT, preferred_element_type=jnp.float32)
             return 0
 
-        lax.fori_loop(0, size, one_c, 0)
+        lax.fori_loop(0, size // GROUP, some_c, 0)
+
+        @pl.when(k + lead < CHUNKS)
+        def _():
+            turn_block(k + lead)
 
         @pl.when(((lax.rem(k, 2) == 1) & (k < CHUNKS - 1)) | (k == CHUNKS - 2))
         def _():
@@ -326,7 +340,7 @@
             pltpu.VMEM((n_c, n_a, whole), jnp.bfloat16),
             pltpu.VMEM((n_b, n_d, whole), jnp.bfloat16),
             pltpu.VMEM((2, pairs, size, n_d), jnp.bfloat16),
-            pltpu.VMEM((size, pairs, n_d), jnp.bfloat16),
+            pltpu.VMEM((CHUNKS // 2, size, pairs, n_d), jnp.bfloat16),
             pltpu.VMEM((size, n_b, n_a, n_d), jnp.bfloat16),
             pltpu.VMEM((pairs, width), jnp.float32),
             pltpu.VMEM((ncol, some, width), jnp.float32),

time: 247 us -> 199 us (0.81)
  Pallas kernels: 241 us -> 193 us
    pallas_call x1, Pallas kernels: 241 us -> 193 us  [on_device(): pl.pallas_call(functools.partial(kernel, ncol, ndev), out_shape=jax.Shape...]
where the time goes in v2:
time: 199 us; the launch traced here: 198 us
  Pallas kernels  193 us (97%)
  local copies, waits for them, and re-layouts  5.72 us (3%)
    pallas_call x1, Pallas kernels, on_device(): pl.pallas_call(functools.partial(kernel, ncol, ndev), out_shape=jax.Shape...  193 us
    unnamed x1, local copies, waits for them, and re-layouts  4.1 us

profile of v2, /device:TPU:0, one launch (start us, length us, event | category | flops | bytes accessed | tf_op | source)
XLA Modules:
  0.0 198.3 jit_solution(6634421963073187282)
XLA Ops:
  0.0 4.1 %copy.7 = bf16[16,128,512]{2,0,1:T(8,128)(2,1)} copy(bf16[16,128,512]{2,1,0:T(8,128)(2,1)} %param.3) | data formatting | bytes 4194304 | tf_op args[0]
  4.1 192.5 %shard_map.37 = f32[16,256]{1,0:T(8,128)} custom-call(bf16[128,16,512]{2,1,0:T(8,128)(2,1)} %bitcast.4, bf16[16,256,256]{2,1,0:T(8,128)(2,1)} %second.1, bf16[512,128,256]{2,1,0:T(8,128)(2,1)} %amps.1), custom_call_target="tpu_custom_call" | custom-call | tf_op jit(solution)/shard_map/pallas_call | solution.py:334
  196.7 0.8 reshape.6
  197.5 0.1 copy.5
  197.6 0.7 reshape.7
